TPU v7x, 32 devices: a whole 2x2x4 slice. The times are simulated.
32 devices in a mesh: grp: 4 (over x, core), sub: 8 (over z, y).
Axes of the slice: x: 2, y: 2, z: 4, core: 2. Of those that a mesh axis runs over, the one named last changes fastest.
Arguments:
- points: bfloat16 [32768, 1024], P(('grp', 'sub')), may hold values from -16 to 16
- level1_ids: int32 [32768], P(('grp', 'sub')), may hold values from 0 to 255
- level2_ids: int32 [32768], P(('grp', 'sub')), may hold values from 0 to 8191, as said below
- level3_ids: int32 [32768], P(('grp', 'sub')), may hold values from 0 to 255
- needed: int32 [32, 32], P(('grp', 'sub')), may hold values from 0 to 8191, as said below
- centroids1: bfloat16 [65536, 1024], P(('grp', 'sub')), may hold values from -6 to 6
- centroids2: bfloat16 [4, 8192, 1024], P('grp', 'sub'), may hold values from -3 to 3
- centroids3: bfloat16 [256, 1024], replicated, may hold values from -6 to 6
Outputs:
- level1_new: float32 [65536, 1024], P(('grp', 'sub'))
- level2_new: float32 [4, 8192, 1024], P('grp', 'sub')
- level3_new: float32 [256, 1024], replicated
Inputs may be any that keep to these rules, and one draw needn't show every extreme that they name: `needed`: each row lists distinct blocks; a row names at most 2 blocks held by one device (blocks of device o are o * 256 to o * 256 + 255), and names exactly 2 of some device's blocks. `level2_ids`: of one device's points, at most 256 have level-2 ids in any one range r * 8192 // 8 to (r + 1) * 8192 // 8 - 1, and exactly 256 in some range.
All inputs are finite; a program needn't handle non-finite values.
Results may differ from a plain program's by a relative error of at most 0.0055.
Values may be sent and summed in bfloat16 or wider, within the bound.
A program may use at most 128 MiB of HBM per device.

v0:
```python
import jax
import jax.numpy as jnp
from jax import lax
from jax.sharding import PartitionSpec as P

D = 1024
K1_DEV = 2048
BLK = 8
CAP = 2
K2 = 8192
K3 = 256


def weighted_hot(labels, count, weights_low):
    return jnp.where(
        labels[:, None] == jnp.arange(count)[None, :],
        weights_low[:, None],
        jnp.zeros((), jnp.bfloat16),
    )


def column_sums(hot_table, points):
    return lax.dot_general(
        hot_table, points, (((0,), (0,)), ((), ())), preferred_element_type=jnp.float32
    )


def shards(points, level1_ids, level2_ids, level3_ids, needed, centroids1, centroids2, centroids3):
    devices = lax.axis_size(("grp", "sub"))
    sub_count = lax.axis_size("sub")
    blocks_dev = K1_DEV // BLK
    wanted = needed[0]
    owners = wanted // blocks_dev
    owner_hits = (owners[:, None] == jnp.arange(devices)[None, :]).astype(jnp.int32)
    places = jnp.sum(jnp.cumsum(owner_hits, axis=0) * owner_hits, axis=1) - 1
    slot_index = owners * CAP + places
    requests = jnp.zeros((devices * CAP,), jnp.int32).at[slot_index].set(wanted % blocks_dev)
    block_table = centroids1.reshape(blocks_dev, BLK * D)
    flat_asked = lax.all_to_all(
        requests.reshape(devices, 1, CAP), ("grp", "sub"), split_axis=0, concat_axis=0, tiled=True
    )[:, 0, :]
    served = lax.all_to_all(
        block_table[flat_asked], ("grp", "sub"), split_axis=0, concat_axis=0, tiled=True
    )
    fetched_rows = served.reshape(devices * CAP * BLK, D)
    matches = (level1_ids[:, None] // BLK == jnp.arange(wanted.shape[0])[None, :]).astype(jnp.int32)
    point_slots = jnp.sum(matches * slot_index[None, :], axis=1)
    row_index = point_slots * BLK + level1_ids % BLK
    nearest = fetched_rows[row_index].astype(jnp.float32)
    values = points.astype(jnp.float32)
    spread = jnp.sum((values - nearest) ** 2, axis=1) / D
    weights_low = (1.0 / (1.0 + spread)).astype(jnp.bfloat16)
    hot_one = weighted_hot(row_index, devices * CAP * BLK, weights_low)
    sums_one = column_sums(hot_one, points)
    mass_one = jnp.sum(hot_one.astype(jnp.float32), axis=0)
    back_sums, back_mass = (
        lax.all_to_all(
            sums_one.reshape(devices, CAP * BLK, D),
            ("grp", "sub"),
            split_axis=0,
            concat_axis=0,
            tiled=True,
        ),
        lax.all_to_all(
            mass_one.reshape(devices, CAP * BLK),
            ("grp", "sub"),
            split_axis=0,
            concat_axis=0,
            tiled=True,
        ),
    )
    owner_hot = (flat_asked.reshape(1, devices * CAP) == jnp.arange(blocks_dev)[:, None]).astype(
        jnp.float32
    )
    gathered = jnp.dot(
        owner_hot, back_sums.reshape(devices * CAP, BLK * D), precision=lax.Precision.HIGHEST
    )
    gathered_mass = jnp.dot(
        owner_hot, back_mass.reshape(devices * CAP, BLK), precision=lax.Precision.HIGHEST
    )
    level1_new = (centroids1.astype(jnp.float32) + gathered.reshape(K1_DEV, D)) / (
        1.0 + gathered_mass.reshape(K1_DEV, 1)
    )
    shard_rows = K2 // sub_count
    capacity = 2 * points.shape[0] // sub_count
    targets = level2_ids // shard_rows
    target_hits = (targets[:, None] == jnp.arange(sub_count)[None, :]).astype(jnp.int32)
    rank_in = jnp.sum(jnp.cumsum(target_hits, axis=0) * target_hits, axis=1) - 1
    send_index = targets * capacity + rank_in
    local_label = level2_ids % shard_rows
    outgoing = jnp.zeros((sub_count * capacity, D), jnp.bfloat16).at[send_index].set(points)
    out_weights = jnp.zeros((sub_count * capacity,), jnp.bfloat16).at[send_index].set(weights_low)
    out_high = (
        jnp.zeros((sub_count * capacity,), jnp.bfloat16)
        .at[send_index]
        .set((local_label // 64).astype(jnp.bfloat16))
    )
    out_low = (
        jnp.zeros((sub_count * capacity,), jnp.bfloat16)
        .at[send_index]
        .set((local_label % 64).astype(jnp.bfloat16))
    )
    got_rows, got_weights, got_high, got_low = (
        lax.all_to_all(
            outgoing.reshape(sub_count, capacity, D), "sub", split_axis=0, concat_axis=0, tiled=True
        ),
        lax.all_to_all(
            out_weights.reshape(sub_count, capacity), "sub", split_axis=0, concat_axis=0, tiled=True
        ),
        lax.all_to_all(
            out_high.reshape(sub_count, capacity), "sub", split_axis=0, concat_axis=0, tiled=True
        ),
        lax.all_to_all(
            out_low.reshape(sub_count, capacity), "sub", split_axis=0, concat_axis=0, tiled=True
        ),
    )
    got_labels = got_high.astype(jnp.float32) * 64.0 + got_low.astype(jnp.float32)
    label_grid = jnp.arange(shard_rows).astype(jnp.float32)[None, None, :]
    hot_route = jnp.where(
        got_labels[:, :, None] == label_grid, got_weights[:, :, None], jnp.zeros((), jnp.bfloat16)
    )
    per_source = jnp.einsum("sck,scd->skd", hot_route, got_rows, preferred_element_type=jnp.float32)
    sums_two = jnp.sum(per_source.astype(jnp.bfloat16).astype(jnp.float32), axis=0)
    source_mass = jnp.sum(hot_route.astype(jnp.float32), axis=1)
    mass_two = jnp.sum(source_mass.astype(jnp.bfloat16).astype(jnp.float32), axis=0)
    level2_new = ((centroids2[0].astype(jnp.float32) + sums_two) / (1.0 + mass_two[:, None]))[None]
    hot_three = weighted_hot(level3_ids, K3, weights_low)
    sums_three, mass_three = lax.psum(
        (column_sums(hot_three, points), jnp.sum(hot_three.astype(jnp.float32), axis=0)),
        ("grp", "sub"),
    )
    level3_new = (centroids3.astype(jnp.float32) + sums_three) / (1.0 + mass_three[:, None])
    return (level1_new, level2_new, level3_new)


def solution(mesh):
    placed = (
        P(("grp", "sub"), None),
        P(("grp", "sub")),
        P(("grp", "sub")),
        P(("grp", "sub")),
        P(("grp", "sub"), None),
        P(("grp", "sub"), None),
        P("grp", "sub", None),
        P(),
    )
    return jax.shard_map(
        shards,
        mesh=mesh,
        in_specs=placed,
        out_specs=(P(("grp", "sub"), None), P("grp", "sub", None), P()),
        check_vma=False,
    )
```

profile of v0, /device:TPU:1, one launch (start us, length us, event | category | flops | bytes accessed | tf_op | source)
XLA Modules:
  0.0 399.0 jit_solution(9396576636143292178)
XLA Ops:
  7.2 0.7 and_select_fusion.1
  8.0 0.2 select_reduce_fusion.1
  8.1 0.7 fusion.43
  8.8 0.7 scatter_custom_fusion
  9.5 0.7 reshape.278
  10.2 7.1 %all-to-all-start = ((s32[32,1,2]{2,1,0:T(1,128)}), s32[32,1,2]{2,1,0:T(1,128)S(1)}, u32[]{:S(2)}, u32[]{:S(2)}) async-start(s32[32,1,2]{2,1,0:T(1,128)} %bitcast.4), calls=%async_computation | async-start | bytes 32768 | tf_op jit(solution)/shard_map/all_to_all | solution.py:39
  17.3 7.4 %reshape.279 = bf16[256,8192]{1,0:T(8,128)(2,1)} reshape(bf16[2048,1024]{1,0:T(8,128)(2,1)} %param.13) | data formatting | bytes 8388608 | tf_op jit(solution)/shard_map/reshape | solution.py:38
  24.8 0.1 copy.31
  24.8 0.1 reshape.289
  25.0 4.9 %gather_fusion = bf16[64,8192]{1,0:T(8,128)(2,1)S(1)} fusion(bf16[256,8192]{1,0:T(8,128)(2,1)} %reshape.279, s32[1024]{0:T(1024)S(1)} %pad_clamp_fusion), kind=kCustom, calls=%fused_computation | custom fusion | bytes 2097408 | tf_op jit(solution)/shard_map/gather | solution.py:43
  29.9 1.5 reshape.288
  31.4 5.8 %all-to-all-start.1 = ((bf16[32,2,8192]{2,1,0:T(2,128)(2,1)}), bf16[32,2,8192]{2,1,0:T(2,128)(2,1)S(1)}, u32[]{:S(2)}, u32[]{:S(2)}) async-start(bf16[32,2,8192]{2,1,0:T(2,128)(2,1)} %reshape.288), calls=%async_computation.1 | async-start | bytes 2097152 | tf_op jit(solution)/shard_map/all_to_all | solution.py:42
  37.3 2.3 reduce-window.6
  39.6 0.3 slice_reduce_fusion
  39.8 0.2 reduce-window.9
  40.0 0.1 add_bitcast_fusion
  40.1 7.6 %scatter_custom_fusion.2 = bf16[2048]{0:T(1024)(128)(2,1)S(1)} fusion(s32[1024]{0:T(1024)S(1)} %compare_select_fusion.2, bf16[1024]{0:T(1024)(128)(2,1)S(1)} %get-tuple-element.6, bf16[]{:T(256)} %constant.131.clone.1), kind=kCustom, calls=%fused_computation.94 | custom fusion | bytes 4098 | tf_op jit(solution)/shard_map/scatter | solution.py:101
  47.7 0.6 broadcast.333
  48.3 0.7 reduce.11
  49.0 0.6 reshape.378
  49.7 7.6 %scatter_custom_fusion.1 = bf16[2048]{0:T(1024)(128)(2,1)S(1)} fusion(s32[1024]{0:T(1024)S(1)} %compare_select_fusion.2, bf16[1024]{0:T(1024)(128)(2,1)S(1)} %get-tuple-element.5, bf16[]{:T(256)} %constant.131.clone.1), kind=kCustom, calls=%fused_computation.96 | custom fusion | bytes 4098 | tf_op jit(solution)/shard_map/scatter | solution.py:96
  57.3 0.7 reduce.12
  58.0 0.6 reshape.380
  58.6 0.1 select_reduce_fusion
  58.7 5.5 %all-to-all-done.1 = bf16[32,2,8192]{2,1,0:T(2,128)(2,1)S(1)} async-done(((bf16[32,2,8192]{2,1,0:T(2,128)(2,1)}), bf16[32,2,8192]{2,1,0:T(2,128)(2,1)S(1)}, u32[]{:S(2)}, u32[]{:S(2)}) %all-to-all-start.1) | async-done | bytes 1048608 | tf_op jit(solution)/shard_map/all_to_all | solution.py:42
  64.2 3.5 all-to-all-start.5
  67.7 0.8 reshape.280
  68.6 4.1 %gather_fusion.1 = bf16[1024,1024]{1,0:T(8,128)(2,1)S(1)} fusion(bf16[512,1024]{1,0:T(8,128)(2,1)S(1)} %reshape.280, s32[1024]{0:T(1024)S(1)} %get-tuple-element.3), kind=kCustom, calls=%fused_computation.1 | custom fusion | bytes 4198400 | tf_op jit(solution)/shard_map/gather | solution.py:49
  72.6 2.3 multiply_reduce_fusion
  75.0 5.4 %all-to-all-start.4 = ((bf16[8,2,128]{2,1,0:T(2,128)(2,1)}), bf16[8,2,128]{2,1,0:T(2,128)(2,1)S(1)}, u32[]{:S(2)}, u32[]{:S(2)}) async-start(bf16[8,2,128]{2,1,0:T(2,128)(2,1)} %reshape.380), calls=%async_computation.4 | async-start | bytes 8192 | tf_op jit(solution)/shard_map/all_to_all | solution.py:110
  80.4 0.3 convert_reduce_fusion.1
  80.7 0.7 all_to_all.39
  81.4 4.2 %all-to-all-done.4 = bf16[8,2,128]{2,1,0:T(2,128)(2,1)S(1)} async-done(((bf16[8,2,128]{2,1,0:T(2,128)(2,1)}), bf16[8,2,128]{2,1,0:T(2,128)(2,1)S(1)}, u32[]{:S(2)}, u32[]{:S(2)}) %all-to-all-start.4) | async-done | bytes 4128 | tf_op jit(solution)/shard_map/all_to_all | solution.py:110
  85.6 4.6 %all-to-all-start.3 = ((f32[32,1,16]{2,1,0:T(1,128)}), f32[32,1,16]{2,1,0:T(1,128)S(1)}, u32[]{:S(2)}, u32[]{:S(2)}) async-start(f32[32,1,16]{2,1,0:T(1,128)} %bitcast.9), calls=%async_computation.3 | async-start | bytes 32768 | tf_op jit(solution)/shard_map/all_to_all | solution.py:64
  90.2 7.6 %scatter_custom_fusion.3 = bf16[2048]{0:T(1024)(128)(2,1)S(1)} fusion(s32[1024]{0:T(1024)S(1)} %compare_select_fusion.2, bf16[1024]{0:T(1024)(128)(2,1)S(1)} %divide_convert_fusion, bf16[]{:T(256)} %constant.131.clone.1), kind=kCustom, calls=%fused_computation.92 | custom fusion | bytes 4098 | tf_op jit(solution)/shard_map/scatter | solution.py:92
  97.8 0.7 reduce.13
  98.6 0.6 reshape.382
  99.2 5.6 %all-to-all-start.6 = ((bf16[8,2,128]{2,1,0:T(2,128)(2,1)}), bf16[8,2,128]{2,1,0:T(2,128)(2,1)S(1)}, u32[]{:S(2)}, u32[]{:S(2)}) async-start(bf16[8,2,128]{2,1,0:T(2,128)(2,1)} %reshape.382), calls=%async_computation.6 | async-start | bytes 8192 | tf_op jit(solution)/shard_map/all_to_all | solution.py:107
  104.7 4.5 %fusion.9 = f32[512,1024]{1,0:T(8,128)} fusion(bf16[1024,1024]{1,0:T(8,128)(2,1)} %param.8, s32[1024]{0:T(1024)S(1)} %get-tuple-element.4, bf16[1024]{0:T(1024)(128)(2,1)S(1)} %divide_convert_fusion), kind=kOutput, calls=%fused_computation.23 | convolution fusion | flops 1074790400 | bytes 4200448 | tf_op jit(solution)/shard_map/dot_general | solution.py:23
  109.2 0.8 all-to-all-done.6
  110.0 5.7 %all-to-all-start.2 = ((f32[32,16,1024]{2,1,0:T(8,128)}), f32[32,16,1024]{2,1,0:T(8,128)}, u32[]{:S(2)}, u32[]{:S(2)}) async-start(f32[32,16,1024]{2,1,0:T(8,128)} %bitcast.77), calls=%async_computation.2 | async-start | bytes 4194304 | tf_op jit(solution)/shard_map/all_to_all | solution.py:57
  115.7 8.0 %scatter_custom_fusion.4 = bf16[2048,1024]{1,0:T(8,128)(2,1)} fusion(s32[1024]{0:T(1024)S(1)} %compare_select_fusion.2, bf16[1024,1024]{1,0:T(8,128)(2,1)S(1)} %copy-done, bf16[]{:T(256)} %constant.131.clone.1), kind=kCustom, calls=%fused_computation.16 | custom fusion | bytes 4194306 | tf_op jit(solution)/shard_map/scatter | solution.py:91
  123.7 41.5 %all-to-all-done.2 = f32[32,16,1024]{2,1,0:T(8,128)} async-done(((f32[32,16,1024]{2,1,0:T(8,128)}), f32[32,16,1024]{2,1,0:T(8,128)}, u32[]{:S(2)}, u32[]{:S(2)}) %all-to-all-start.2) | async-done | bytes 2097184 | tf_op jit(solution)/shard_map/all_to_all | solution.py:57
  165.2 4.7 %all-to-all-start.7 = ((bf16[8,256,1024]{2,1,0:T(8,128)(2,1)}), bf16[8,256,1024]{2,1,0:T(8,128)(2,1)}, u32[]{:S(2)}, u32[]{:S(2)}) async-start(bf16[8,256,1024]{2,1,0:T(8,128)(2,1)} %bitcast.76), calls=%async_computation.7 | async-start | bytes 8388608 | tf_op jit(solution)/shard_map/all_to_all | solution.py:104
  170.0 0.5 broadcast.330
  170.5 0.7 reduce.9
  171.2 0.1 eq.112
  171.4 2.0 fusion.13
  173.4 0.3 convert_reduce_fusion.2
  173.8 115.0 %psum.15 = f32[256]{0:T(256)S(1)} all-reduce(f32[256]{0:T(256)S(1)} %convert_reduce_fusion.2), channel_id=1, replica_groups=mesh['grp'=4,'sub'=8] {'grp','sub'}, use_global_device_ids=true, to_apply=%region_18.19 | all-reduce | flops 256 | bytes 2048 | tf_op jit(solution)/shard_map/psum | solution.py:128
  288.8 0.5 broadcast.331
  289.3 0.7 reduce.10
  290.1 0.2 convolution_add_fusion
  290.2 0.2 copy.33
  290.4 0.1 add.187
  290.6 1.3 fusion
  291.9 63.0 %all-reduce.2.cloned.1.call-done = f32[256,1024]{1,0:T(8,128)} async-done(((f32[256,1024]{1,0:T(8,128)}), f32[256,1024]{1,0:T(8,128)}) %all-reduce.2.cloned.1.call-update) | async-done | bytes 1048592 | tf_op jit(solution)/shard_map/psum | solution.py:128
  354.9 2.4 add_divide_fusion.1
  357.3 1.7 reshape.282
  359.0 5.7 %fusion.20 = f32[256,8192]{1,0:T(8,128)} fusion(f32[64,8192]{1,0:T(8,128)S(1)} %reshape.282, s32[64]{0:T(128)S(1)} %eq.112), kind=kOutput, calls=%fused_computation.39 | convolution fusion | flops 1610629120 | bytes 10486016 | tf_op jit(solution)/shard_map/dot_general | solution.py:75
  364.7 9.4 %reshape.283 = f32[2048,1024]{1,0:T(8,128)} reshape(f32[256,8192]{1,0:T(8,128)} %fusion.20) | data formatting | bytes 16777216 | tf_op jit(solution)/shard_map/reshape | solution.py:81
  374.0 7.7 %add_divide_fusion = f32[2048,1024]{1,0:T(8,128)} fusion(f32[2048,1024]{1,0:T(8,128)} %reshape.283, bf16[2048,1024]{1,0:T(8,128)(2,1)} %param.13, f32[2048]{0:T(1024)S(1)} %add.187), kind=kLoop, calls=%fused_computation.8 | loop fusion | flops 6291456 | bytes 20979712 | tf_op jit(solution)/shard_map/div | solution.py:81
  381.7 7.6 %convert_reduce_fusion = f32[1024,1024]{1,0:T(8,128)S(1)} fusion(bf16[8,256,1024]{2,1,0:T(8,128)(2,1)} %all-to-all-done.7, f32[8,256]{1,0:T(8,128)S(1)} %bitcast.80, f32[1024]{0:T(1024)S(1)} %iota_convert_fusion, bf16[8,256]{1,0:T(8,128)(2,1)S(1)} %bitcast.83), kind=kOutput, calls=%fused_computation.7 | convolution fusion | flops 4323278848 | bytes 8404992 | tf_op jit(solution)/shard_map/sck,scd->skd/dot_general | solution.py:122
  389.3 2.8 fusion.1
  (47 shorter events, 0.6 us)
Async XLA Ops:
  10.2 14.5 %all-to-all-start = ((s32[32,1,2]{2,1,0:T(1,128)}), s32[32,1,2]{2,1,0:T(1,128)S(1)}, u32[]{:S(2)}, u32[]{:S(2)}) async-start(s32[32,1,2]{2,1,0:T(1,128)} %bitcast.4), calls=%async_computation | async-start | bytes 32768 | tf_op jit(solution)/shard_map/all_to_all | solution.py:39
  29.9 7.4 %copy-start.5 = (s32[1024]{0:T(1024)S(1)}, s32[1024]{0:T(1024)}, u32[]{:S(2)}) copy-start(s32[1024]{0:T(1024)} %param.10) | copy-start | bytes 12292
  29.9 28.7 %copy-start.6 = (s32[1,32]{1,0:T(1,128)S(1)}, s32[1,32]{1,0:T(1,128)}, u32[]{:S(2)}) copy-start(s32[1,32]{1,0:T(1,128)} %param.12) | copy-start | bytes 388
  29.9 28.7 %copy-start.4 = (s32[1024]{0:T(1024)S(1)}, s32[1024]{0:T(1024)}, u32[]{:S(2)}) copy-start(s32[1024]{0:T(1024)} %param.9) | copy-start | bytes 12292
  31.4 32.8 %all-to-all-start.1 = ((bf16[32,2,8192]{2,1,0:T(2,128)(2,1)}), bf16[32,2,8192]{2,1,0:T(2,128)(2,1)S(1)}, u32[]{:S(2)}, u32[]{:S(2)}) async-start(bf16[32,2,8192]{2,1,0:T(2,128)(2,1)} %reshape.288), calls=%async_computation.1 | async-start | bytes 2097152 | tf_op jit(solution)/shard_map/all_to_all | solution.py:42
  64.2 10.8 %all-to-all-start.5 = ((bf16[8,2,128]{2,1,0:T(2,128)(2,1)}), bf16[8,2,128]{2,1,0:T(2,128)(2,1)S(1)}, u32[]{:S(2)}, u32[]{:S(2)}) async-start(bf16[8,2,128]{2,1,0:T(2,128)(2,1)} %reshape.378), calls=%async_computation.5 | async-start | bytes 8192 | tf_op jit(solution)/shard_map/all_to_all | solution.py:113
  75.0 10.6 %all-to-all-start.4 = ((bf16[8,2,128]{2,1,0:T(2,128)(2,1)}), bf16[8,2,128]{2,1,0:T(2,128)(2,1)S(1)}, u32[]{:S(2)}, u32[]{:S(2)}) async-start(bf16[8,2,128]{2,1,0:T(2,128)(2,1)} %reshape.380), calls=%async_computation.4 | async-start | bytes 8192 | tf_op jit(solution)/shard_map/all_to_all | solution.py:110
  85.6 13.5 %all-to-all-start.3 = ((f32[32,1,16]{2,1,0:T(1,128)}), f32[32,1,16]{2,1,0:T(1,128)S(1)}, u32[]{:S(2)}, u32[]{:S(2)}) async-start(f32[32,1,16]{2,1,0:T(1,128)} %bitcast.9), calls=%async_computation.3 | async-start | bytes 32768 | tf_op jit(solution)/shard_map/all_to_all | solution.py:64
  99.2 10.8 %all-to-all-start.6 = ((bf16[8,2,128]{2,1,0:T(2,128)(2,1)}), bf16[8,2,128]{2,1,0:T(2,128)(2,1)S(1)}, u32[]{:S(2)}, u32[]{:S(2)}) async-start(bf16[8,2,128]{2,1,0:T(2,128)(2,1)} %reshape.382), calls=%async_computation.6 | async-start | bytes 8192 | tf_op jit(solution)/shard_map/all_to_all | solution.py:107
  104.7 11.0 %copy-start = (bf16[1024,1024]{1,0:T(8,128)(2,1)S(1)}, bf16[1024,1024]{1,0:T(8,128)(2,1)}, u32[]{:S(2)}) copy-start(bf16[1024,1024]{1,0:T(8,128)(2,1)} %param.8) | copy-start | bytes 6291460
  110.0 55.2 %all-to-all-start.2 = ((f32[32,16,1024]{2,1,0:T(8,128)}), f32[32,16,1024]{2,1,0:T(8,128)}, u32[]{:S(2)}, u32[]{:S(2)}) async-start(f32[32,16,1024]{2,1,0:T(8,128)} %bitcast.77), calls=%async_computation.2 | async-start | bytes 4194304 | tf_op jit(solution)/shard_map/all_to_all | solution.py:57
  165.2 6.2 %copy-start.3 = (s32[1024]{0:T(1024)S(1)}, s32[1024]{0:T(1024)}, u32[]{:S(2)}) copy-start(s32[1024]{0:T(1024)} %param.11) | copy-start | bytes 12292
  165.2 216.5 %all-to-all-start.7 = ((bf16[8,256,1024]{2,1,0:T(8,128)(2,1)}), bf16[8,256,1024]{2,1,0:T(8,128)(2,1)}, u32[]{:S(2)}, u32[]{:S(2)}) async-start(bf16[8,256,1024]{2,1,0:T(8,128)(2,1)} %bitcast.76), calls=%async_computation.7 | async-start | bytes 8388608 | tf_op jit(solution)/shard_map/all_to_all | solution.py:104
  169.9 184.9 %copy-start.2 = (bf16[256,1024]{1,0:T(8,128)(2,1)S(1)}, bf16[256,1024]{1,0:T(8,128)(2,1)}, u32[]{:S(2)}) copy-start(bf16[256,1024]{1,0:T(8,128)(2,1)} %param.15) | copy-start | bytes 1572868
  170.0 184.9 %all-reduce.2.cloned.1.call-start = ((), (), s32[]{:S(2)}) async-start(), calls=%async_computation.8 | async-start | bytes 2097152 | tf_op jit(solution)/shard_map/psum | solution.py:128
  381.7 7.6 %copy-start.1 = (bf16[1,1024,1024]{2,1,0:T(8,128)(2,1)S(1)}, bf16[1,1024,1024]{2,1,0:T(8,128)(2,1)}, u32[]{:S(2)}) copy-start(bf16[1,1024,1024]{2,1,0:T(8,128)(2,1)} %param.14) | copy-start | bytes 6291460
Sparse Core Ops, SparseCore 0:
  176.5 178.3 all-reduce.1
where the time goes:
time: 402 us; the launch traced here: 399 us
  waiting for transfers between devices  115 us (29%)
  blocking collectives  115 us (29%)
  local copies, waits for them, and re-layouts  67.1 us (17%)
  starting transfers between devices  42.4 us (11%)
  other arithmetic  25.1 us (6%)
  matrix products  19.8 us (5%)
  between operations  14.4 us (4%)
    psum x1, blocking collectives, shards(): lax.psum((column_sums(hot_three, points), jnp.sum(hot_three.astype(jnp.fl...  115 us
    psum x1, waiting for transfers between devices, shards(): lax.psum((column_sums(hot_three, points), jnp.sum(hot_three.astype(jnp.fl...  63 us
    all_to_all x1, waiting for transfers between devices, shards(): lax.all_to_all(sums_one.reshape(devices, CAP * BLK, D), ('grp', 'sub'), s...  41.5 us
    reshape x1, local copies, waits for them, and re-layouts, shards(): gathered.reshape(K1_DEV, D)  9.39 us
  transfers between devices with their start and end apart: 9, of which 5 were waited for; matrix products, arithmetic and copies ran while one was open for 23% of the time, Pallas kernels for 0%

commit v1 on v0

v1 whole, which is shorter than its diff:
```python
import functools

import jax
import jax.numpy as jnp
from jax import lax
from jax.experimental import pallas as pl
from jax.experimental.pallas import tpu as pltpu
from jax.sharding import PartitionSpec as P

BLK = 8
CAP = 2
LANES = 128
MESH = pl.DeviceIdType.MESH
F32 = jnp.float32
BF16 = jnp.bfloat16


def iota(shape, dim):
    return lax.broadcasted_iota(jnp.int32, shape, dim)


def step_kernel(
    groups,
    subs,
    served,
    points,
    pidx_col,
    pidx_row,
    sidx_row,
    l3_row,
    lrows,
    cent3,
    back_out,
    l2_out,
    meta_out,
    l3_out,
    fetched,
    back_src,
    l2_src,
    meta_src,
    w_row,
    a_src,
    a_dst,
    b_src,
    b_dst,
    c_buf,
    e1s,
    e1r,
    e3s,
    e3r,
    l2s,
    l2r,
    ms,
    mr,
    as_,
    ar,
    bs,
    br,
    cs,
    cr,
    ds_,
    dr,
    lsem,
):
    n = groups * subs
    g_me, s_me = lax.axis_index("grp"), lax.axis_index("sub")
    me = g_me * subs + s_me
    slots = CAP * BLK
    pts, feat = points.shape
    cap = l2_src.shape[1]
    rows_a = a_src.shape[1]
    rows_b = b_src.shape[1]

    def flat(k):
        t = lax.rem(me + k, n)
        return (lax.div(t, subs), lax.rem(t, subs))

    def sub_peer(k):
        return lax.rem(s_me + k, subs)

    def grp_peer(k):
        return lax.rem(g_me + k, groups)

    barrier = pltpu.get_barrier_semaphore()

    @pl.loop(1, n)
    def _(k):
        pl.semaphore_signal(barrier, inc=1, device_id=flat(k), device_id_type=MESH)

    pl.semaphore_wait(barrier, n - 1)

    def remote(src, dst, ss, rs, dev):
        return pltpu.make_async_remote_copy(
            src_ref=src, dst_ref=dst, send_sem=ss, recv_sem=rs, device_id=dev, device_id_type=MESH
        )

    def e1(k):
        t = lax.rem(me + k, n)
        return remote(served.at[t], fetched.at[me], e1s.at[k], e1r.at[k], flat(k))

    def e3(k):
        t = lax.rem(me + k, n)
        return remote(back_src.at[t], back_out.at[me], e3s.at[k], e3r.at[k], flat(k))

    def e2(k):
        t = sub_peer(k)
        return remote(l2_src.at[t], l2_out.at[s_me], l2s.at[k], l2r.at[k], (g_me, t))

    def em(k):
        t = sub_peer(k)
        return remote(meta_src.at[t], meta_out.at[s_me], ms.at[k], mr.at[k], (g_me, t))

    def ea(k):
        t = grp_peer(k)
        return remote(a_src.at[t], a_dst.at[g_me], as_.at[k], ar.at[k], (t, s_me))

    def eb(k):
        t = sub_peer(k)
        return remote(b_src.at[t], b_dst.at[s_me], bs.at[k], br.at[k], (g_me, t))

    def ec(k):
        t = sub_peer(k)
        return remote(c_buf.at[s_me], c_buf.at[s_me], cs.at[k], cr.at[k], (g_me, t))

    def ed(k):
        t = grp_peer(k)
        return remote(c_buf, l3_out.at[g_me], ds_.at[k], dr.at[k], (t, s_me))

    @pl.loop(1, n)
    def _(k):
        e1(k).start()

    fetched[me] = served[me]

    def route(t):
        slot = iota((cap, pts), 0) + t * cap
        return jnp.where(sidx_row[...] == slot, F32(1), F32(0)).astype(BF16)

    def build(k):
        t = sub_peer(k)
        l2_src[t] = jnp.dot(route(t), points[...], preferred_element_type=F32).astype(BF16)

    half = subs // 2

    @pl.loop(1, half)
    def _(k):
        build(k)
        e2(k).start()

    @pl.loop(1, n)
    def _(k):
        e1(k).wait_recv()

    tile = LANES
    total = n * slots

    @pl.loop(0, pts // tile)
    def _(i):
        at = pl.ds(pl.multiple_of(i * tile, tile), tile)
        hot = jnp.where(pidx_col[at, :] == iota((tile, total), 1), F32(1), F32(0)).astype(BF16)
        near = jnp.dot(hot, fetched[...].reshape(total, feat), preferred_element_type=F32)
        diff = points[at, :].astype(F32) - near
        spread = jnp.sum(diff * diff, axis=1, keepdims=True) / feat
        w = (1.0 / (1.0 + spread)).astype(BF16).astype(F32)
        eye = iota((tile, tile), 0) == iota((tile, tile), 1)
        w_row[:, at] = jnp.sum(jnp.where(eye, w, F32(0)), axis=0, keepdims=True)

    per = tile // slots

    def sums(labels, base):
        hot = jnp.where(labels == iota((tile, pts), 0) + base, w_row[...], F32(0))
        mass = jnp.sum(hot, axis=1, keepdims=True)
        return jnp.dot(hot.astype(BF16), points[...], preferred_element_type=F32), mass

    @pl.loop(0, total // tile)
    def _(i):
        s, m = sums(pidx_row[...], i * tile)
        at = pl.ds(i * per, per)
        back_src[at, :, :feat] = s.astype(BF16).reshape(per, slots, feat)
        back_src[at, :, feat:] = (
            jnp.broadcast_to(m, (tile, LANES)).astype(BF16).reshape(per, slots, LANES)
        )

    @pl.loop(1, n)
    def _(k):
        e3(k).start()

    own_back = pltpu.make_async_copy(back_src.at[me], back_out.at[me], lsem.at[0])
    own_back.start()

    k3 = groups * rows_a
    tile3 = min(tile, rows_a)
    for j in range(k3 // tile3):
        hot = jnp.where(l3_row[...] == iota((tile3, pts), 0) + j * tile3, w_row[...], F32(0))
        m = jnp.sum(hot, axis=1, keepdims=True)
        s = jnp.dot(hot.astype(BF16), points[...], preferred_element_type=F32)
        g, r = (j * tile3) // rows_a, (j * tile3) % rows_a
        a_src[g, r : r + tile3, :feat] = s.astype(BF16)
        a_src[g, r : r + tile3, feat:] = jnp.broadcast_to(m, (tile3, LANES)).astype(BF16)
    for k in range(1, groups):
        ea(k).start()

    meta_rows = jnp.where(iota((8, pts), 0) == 0, w_row[...], lrows[...]).astype(BF16)

    def meta(k):
        t = sub_peer(k)
        meta_src[t] = lax.dot_general(
            meta_rows, route(t), (((1,), (1,)), ((), ())), preferred_element_type=F32
        )

    @pl.loop(half, subs)
    def _(k):
        build(k)
        e2(k).start()

    build(0)
    own_l2 = pltpu.make_async_copy(l2_src.at[s_me], l2_out.at[s_me], lsem.at[1])
    own_l2.start()

    for k in range(1, groups):
        ea(k).wait_recv()
    a_dst[g_me] = a_src[g_me]
    acc = a_dst[0].astype(F32)
    for j in range(1, groups):
        acc = acc + a_dst[j].astype(F32)
    for j in range(subs):
        b_src[j] = acc[j * rows_b : (j + 1) * rows_b, :]
    for k in range(1, subs):
        eb(k).start()

    @pl.loop(1, subs)
    def _(k):
        meta(k)
        em(k).start()

    meta(0)
    own_meta = pltpu.make_async_copy(meta_src.at[s_me], meta_out.at[s_me], lsem.at[2])
    own_meta.start()

    for k in range(1, subs):
        eb(k).wait_recv()
    b_dst[s_me] = b_src[s_me]
    acc = b_dst[0]
    for j in range(1, subs):
        acc = acc + b_dst[j]
    c_buf[s_me] = (cent3[g_me, s_me] + acc[:, :feat]) / (1.0 + acc[:, feat : feat + 1])
    for k in range(1, subs):
        ec(k).start()
    for k in range(1, subs):
        ec(k).wait_recv()
    for k in range(1, groups):
        ed(k).start()
    own_l3 = pltpu.make_async_copy(c_buf, l3_out.at[g_me], lsem.at[3])
    own_l3.start()

    own_back.wait()
    own_l2.wait()
    own_meta.wait()
    own_l3.wait()
    for k in range(1, groups):
        ed(k).wait_recv()

    @pl.loop(1, n)
    def _(k):
        e3(k).wait_recv()
        e3(k).wait_send()
        e1(k).wait_send()

    @pl.loop(1, subs)
    def _(k):
        e2(k).wait_recv()
        em(k).wait_recv()
        e2(k).wait_send()
        em(k).wait_send()
        eb(k).wait_send()
        ec(k).wait_send()

    for k in range(1, groups):
        ea(k).wait_send()
        ed(k).wait_send()


def level1_kernel(rows, target, back, cent, out):
    feat = cent.shape[1]
    base = pl.program_id(0) * rows
    hot = jnp.where(
        target[...] == iota((rows, target.shape[1]), 0) + base, F32(1), F32(0)
    ).astype(BF16)
    got = jnp.dot(hot, back[...], preferred_element_type=F32)
    out[...] = (cent[...].astype(F32) + got[:, :feat]) / (1.0 + got[:, feat : feat + 1])


def level2_kernel(rows, labels, weights, got, cent, out):
    base = pl.program_id(0) * rows
    hot = jnp.where(
        labels[...] == iota((rows, labels.shape[1]), 0) + base, weights[...], F32(0)
    )
    mass = jnp.sum(hot, axis=1, keepdims=True)
    sums = jnp.dot(hot.astype(BF16), got[...], preferred_element_type=F32)
    out[...] = (cent[...].astype(F32) + sums) / (1.0 + mass)


def ranks(hits):
    return jnp.sum(jnp.cumsum(hits, axis=0) * hits, axis=1) - 1


def shards(points, level1_ids, level2_ids, level3_ids, needed, centroids1, centroids2, centroids3, *, k2):
    groups, subs = lax.axis_size("grp"), lax.axis_size("sub")
    n = groups * subs
    pts, feat = points.shape
    k1_dev = centroids1.shape[0]
    k3 = centroids3.shape[0]
    blocks_dev = k1_dev // BLK
    slots = CAP * BLK
    need = needed.shape[1]
    wide = feat + LANES

    wanted = needed[0]
    owners = wanted // blocks_dev
    same = owners[:, None] == owners[None, :]
    before = jnp.arange(need)[None, :] < jnp.arange(need)[:, None]
    places = jnp.sum((same & before).astype(jnp.int32), axis=1)
    slot_index = owners * CAP + places
    requests = jnp.sum(
        jnp.where(
            slot_index[None, :] == jnp.arange(n * CAP)[:, None], (wanted % blocks_dev)[None, :], 0
        ),
        axis=1,
    )
    asked = lax.all_to_all(
        requests.reshape(n, CAP), ("grp", "sub"), split_axis=0, concat_axis=0, tiled=True
    )
    target = (asked.reshape(n * CAP, 1) * BLK + jnp.arange(BLK)[None, :]).reshape(n * slots)
    served = centroids1[target].reshape(n, slots, feat)

    entry = level1_ids // BLK
    point_slots = jnp.sum(
        jnp.where(entry[:, None] == jnp.arange(need)[None, :], slot_index[None, :], 0), axis=1
    )
    row_index = point_slots * BLK + level1_ids % BLK

    shard_rows = k2 // subs
    cap = 2 * pts // subs
    range_of = level2_ids // shard_rows
    hits = (range_of[:, None] == jnp.arange(subs)[None, :]).astype(jnp.int32)
    send_index = range_of * cap + ranks(hits)
    local = level2_ids % shard_rows
    lrows = (
        jnp.zeros((8, pts), F32)
        .at[1].set((local // 64).astype(F32))
        .at[2].set((local % 64).astype(F32))
    )

    rows_a = k3 // groups
    rows_b = rows_a // subs
    cent3 = centroids3.astype(F32).reshape(groups, subs, rows_b, feat)
    vmem = pl.BlockSpec(memory_space=pltpu.VMEM)
    anywhere = pl.BlockSpec(memory_space=pl.ANY)
    dma = pltpu.SemaphoreType.DMA
    back, routed, meta, l3 = pl.pallas_call(
        functools.partial(step_kernel, groups, subs),
        out_shape=(
            jax.ShapeDtypeStruct((n, slots, wide), BF16),
            jax.ShapeDtypeStruct((subs, cap, feat), BF16),
            jax.ShapeDtypeStruct((subs, 8, cap), F32),
            jax.ShapeDtypeStruct((groups, subs, rows_b, feat), F32),
        ),
        in_specs=[vmem] * 8,
        out_specs=[anywhere] * 4,
        scratch_shapes=[
            pltpu.VMEM((n, slots, feat), BF16),
            pltpu.VMEM((n, slots, wide), BF16),
            pltpu.VMEM((subs, cap, feat), BF16),
            pltpu.VMEM((subs, 8, cap), F32),
            pltpu.VMEM((1, pts), F32),
            pltpu.VMEM((groups, rows_a, wide), BF16),
            pltpu.VMEM((groups, rows_a, wide), BF16),
            pltpu.VMEM((subs, rows_b, wide), F32),
            pltpu.VMEM((subs, rows_b, wide), F32),
            pltpu.VMEM((subs, rows_b, feat), F32),
            dma((n,)), dma((n,)), dma((n,)), dma((n,)),
            dma((subs,)), dma((subs,)), dma((subs,)), dma((subs,)),
            dma((groups,)), dma((groups,)),
            dma((subs,)), dma((subs,)), dma((subs,)), dma((subs,)),
            dma((groups,)), dma((groups,)),
            dma((4,)),
        ],
        compiler_params=pltpu.CompilerParams(
            collective_id=0, has_side_effects=True, vmem_limit_bytes=56 * 1024 * 1024
        ),
        name="step",
    )(
        served,
        points,
        row_index[:, None],
        row_index[None, :],
        send_index[None, :],
        level3_ids[None, :],
        lrows,
        cent3,
    )

    def tiled(rows, cols):
        return pl.BlockSpec((rows, cols), lambda i: (i, 0))

    def whole(rows, cols):
        return pl.BlockSpec((rows, cols), lambda i: (0, 0))

    tile1 = min(256, k1_dev)
    level1_new = pl.pallas_call(
        functools.partial(level1_kernel, tile1),
        grid=(k1_dev // tile1,),
        in_specs=[whole(1, n * slots), whole(n * slots, wide), tiled(tile1, feat)],
        out_specs=tiled(tile1, feat),
        out_shape=jax.ShapeDtypeStruct((k1_dev, feat), F32),
        name="level1",
    )(target[None, :], back.reshape(n * slots, wide), centroids1)

    labels = (meta[:, 1, :] * 64.0 + meta[:, 2, :]).astype(jnp.int32).reshape(1, subs * cap)
    weights = meta[:, 0, :].reshape(1, subs * cap)
    tile2 = min(256, shard_rows)
    level2_new = pl.pallas_call(
        functools.partial(level2_kernel, tile2),
        grid=(shard_rows // tile2,),
        in_specs=[
            whole(1, subs * cap),
            whole(1, subs * cap),
            whole(subs * cap, feat),
            tiled(tile2, feat),
        ],
        out_specs=tiled(tile2, feat),
        out_shape=jax.ShapeDtypeStruct((shard_rows, feat), F32),
        name="level2",
    )(labels, weights, routed.reshape(subs * cap, feat), centroids2[0])
    return level1_new, level2_new[None], l3.reshape(k3, feat)


def solution(mesh):
    placed = (
        P(("grp", "sub"), None),
        P(("grp", "sub")),
        P(("grp", "sub")),
        P(("grp", "sub")),
        P(("grp", "sub"), None),
        P(("grp", "sub"), None),
        P("grp", "sub", None),
        P(),
    )

    def run(*args):
        return jax.shard_map(
            functools.partial(shards, k2=args[6].shape[1]),
            mesh=mesh,
            in_specs=placed,
            out_specs=(P(("grp", "sub"), None), P("grp", "sub", None), P()),
            check_vma=False,
        )(*args)

    return run
```

time: 402 us -> 255 us (0.63)
  Pallas kernels: 0 us -> 226 us
  blocking collectives: 115 us -> 0 us
  waiting for transfers between devices: 115 us -> 0.01 us
  local copies, waits for them, and re-layouts: 67.1 us -> 10.2 us
  starting transfers between devices: 42.4 us -> 7.08 us
  matrix products: 19.8 us -> 0 us
  other arithmetic: 25.1 us -> 10.8 us
  between operations: 14.4 us -> 0.72 us
    pallas_call x0 -> x3, Pallas kernels: none -> 226 us  [the longest x1 207 us: shards(): pl.pallas_call(functools.partial(step_kernel, groups, subs), out_shape=(j...]
    psum x1 -> x0, blocking collectives: 115 us -> none  [shards(): lax.psum((column_sums(hot_three, points), jnp.sum(hot_three.astype(jnp.fl...]
    psum x1 -> x0, waiting for transfers between devices: 63 us -> none  [shards(): lax.psum((column_sums(hot_three, points), jnp.sum(hot_three.astype(jnp.fl...]
    all_to_all x8 -> x1, waiting for transfers between devices: 52.1 us -> 0.01 us  [shards(): lax.all_to_all(requests.reshape(n, CAP), ('grp', 'sub'), split_axis=0, co...]
    all_to_all x8 -> x1, starting transfers between devices: 42.3 us -> 7.08 us  [shards(): lax.all_to_all(requests.reshape(n, CAP), ('grp', 'sub'), split_axis=0, co...]
    scatter x5 -> x2, local copies, waits for them, and re-layouts: 31.4 us -> 0.12 us  [shards(): lrows = jnp.zeros((8, pts), F32).at[1].set((local // 64).astype(F32)).at[...]
    reshape x6 -> x0, local copies, waits for them, and re-layouts: 20.1 us -> none  [the longest x1 9.39 us: shards(): gathered.reshape(K1_DEV, D)]
    dot_general x5 -> x0, matrix products: 19.8 us -> none  [the longest x1 7.57 us: shards(): jnp.einsum('sck,scd->skd', hot_route, got_rows, preferred_element_type=jn...]
  transfers between devices with their start and end apart: 9 -> 1, of which waited for: 5 -> 0; matrix products, arithmetic and copies ran while one was open for 23% -> 3% of each run, Pallas kernels for 0% -> 0%
where the time goes in v1:
time: 255 us; the launch traced here: 254 us
  Pallas kernels  226 us (89%)
  other arithmetic  10.8 us (4%)
  local copies, waits for them, and re-layouts  10.2 us (4%)
  starting transfers between devices  7.08 us (3%)
    pallas_call x1, Pallas kernels, shards(): pl.pallas_call(functools.partial(step_kernel, groups, subs), out_shape=(j...  207 us
    pallas_call x1, Pallas kernels, shards(): pl.pallas_call(functools.partial(level1_kernel, tile1), grid=(k1_dev // t...  9.89 us
    pallas_call x1, Pallas kernels, shards(): pl.pallas_call(functools.partial(level2_kernel, tile2), grid=(shard_rows...  8.76 us
    all_to_all x1, starting transfers between devices, shards(): lax.all_to_all(requests.reshape(n, CAP), ('grp', 'sub'), split_axis=0, co...  7.08 us
    gather x1, local copies, waits for them, and re-layouts, shards(): served = centroids1[target].reshape(n, slots, feat)  6.2 us
  transfers between devices with their start and end apart: 1, of which 0 were waited for; matrix products, arithmetic and copies ran while one was open for 3% of the time, Pallas kernels for 0%

profile of v1, /device:TPU:1, one launch (start us, length us, event | category | flops | bytes accessed | tf_op | source)
XLA Modules:
  0.0 254.3 jit_solution(15532793985021312438)
XLA Ops:
  0.6 0.7 and_select_fusion.1
  1.3 0.7 and_select_fusion.2
  2.0 0.2 convert_reduce_fusion
  2.1 0.1 select_reduce_fusion.1
  2.2 0.7 all_to_all.6
  3.0 7.1 %all-to-all-start = ((s32[32,1,2]{2,1,0:T(1,128)}), s32[32,1,2]{2,1,0:T(1,128)S(1)}, u32[]{:S(2)}, u32[]{:S(2)}) async-start(s32[32,1,2]{2,1,0:T(1,128)} %bitcast.5), calls=%async_computation | async-start | bytes 32768 | tf_op jit(solution)/shard_map/all_to_all | solution.py:330
  10.1 0.7 add_select_fusion.5
  10.8 0.1 select_reduce_fusion
  10.8 0.7 fusion.4
  11.5 0.0 copy-start.2
  11.5 0.7 fusion.6
  12.3 2.3 reduce-window.6
  14.5 0.3 slice_reduce_fusion
  14.8 0.2 reduce-window.9
  15.0 0.1 add_bitcast_fusion
  15.1 0.6 add_add_fusion
  15.7 1.0 copy.15.pidx_col
  16.7 2.1 convert.1.cent3
  18.9 0.1 scatter.9.lrows
  19.0 0.0 copy-start.1
  19.0 0.0 all-to-all-done
  19.1 0.1 mul.52
  19.2 0.1 iota_add_fusion
  19.2 0.1 add.112
  19.3 0.7 add.111.target
  20.0 6.2 %gather_fusion = bf16[512,1024]{1,0:T(8,128)(2,1)} fusion(bf16[2048,1024]{1,0:T(8,128)(2,1)} %cent.1, s32[1024]{0:T(1024)S(1)} %pad_clamp_fusion), kind=kCustom, calls=%fused_computation | custom fusion | bytes 2099200 | tf_op jit(solution)/shard_map/gather | solution.py:334
  26.2 0.0 copy-done.2
  26.2 0.0 copy-done.1
  26.2 206.9 %step.1 = (bf16[32,16,1152]{2,1,0:T(8,128)(2,1)}, bf16[8,256,1024]{2,1,0:T(8,128)(2,1)}, f32[8,8,256]{2,1,0:T(8,128)}, f32[4,8,8,1024]{3,2,1,0:T(8,128)}) custom-call(bf16[32,16,1024]{2,1,0:T(8,128)(2,1)} %bitcast.53, bf16[1024,1024]{1,0:T(8,128)(2,1)} %points.1, s32[1024,1]{1,0:T(8,128)} %copy.15.pidx_col, s32[1,1024]{1,0:T(1,128)} %bitcast.60, ...), custom_call_target="tpu_custom_call" | custom-call | tf_op jit(solution)/shard_map/step/pallas_call | solution.py:360
  233.1 1.6 fusion.15
  234.7 9.9 %level1.1 = f32[2048,1024]{1,0:T(8,128)} custom-call(s32[1,512]{1,0:T(1,128)} %add.111.target, bf16[512,1152]{1,0:T(8,128)(2,1)} %bitcast.55, bf16[2048,1024]{1,0:T(8,128)(2,1)} %cent.1), custom_call_target="tpu_custom_call" | custom-call | tf_op jit(solution)/shard_map/level1/pallas_call | solution.py:410
  244.6 0.0 copy-start
  244.6 8.8 %level2.1 = f32[1024,1024]{1,0:T(8,128)} custom-call(s32[1,2048]{1,0:T(1,128)} %bitcast.62, f32[1,2048]{1,0:T(1,128)} %bitcast.61, bf16[2048,1024]{1,0:T(8,128)(2,1)} %bitcast.51, bf16[1024,1024]{1,0:T(8,128)(2,1)} %bitcast.54), custom_call_target="tpu_custom_call" | custom-call | tf_op jit(solution)/shard_map/level2/pallas_call | solution.py:422
  253.3 0.0 copy-done
  253.3 1.0 copy.20
  (7 shorter events, 0.1 us)
Async XLA Ops:
  3.0 16.0 %all-to-all-start = ((s32[32,1,2]{2,1,0:T(1,128)}), s32[32,1,2]{2,1,0:T(1,128)S(1)}, u32[]{:S(2)}, u32[]{:S(2)}) async-start(s32[32,1,2]{2,1,0:T(1,128)} %bitcast.5), calls=%async_computation | async-start | bytes 32768 | tf_op jit(solution)/shard_map/all_to_all | solution.py:330
  11.5 14.7 %copy-start.2 = (s32[1024]{0:T(1024)}, s32[1024]{0:T(1024)S(1)}, u32[]{:S(2)}) copy-start(s32[1024]{0:T(1024)S(1)} %fusion.4) | copy-start | bytes 12292
  19.0 7.2 %copy-start.1 = (f32[8,1024]{1,0:T(8,128)}, f32[8,1024]{1,0:T(8,128)S(1)}, u32[]{:S(2)}) copy-start(f32[8,1024]{1,0:T(8,128)S(1)} %scatter.9.lrows) | copy-start | bytes 98308
  244.6 8.8 %copy-start = (f32[4,8,8,1024]{3,2,1,0:T(8,128)S(1)}, f32[4,8,8,1024]{3,2,1,0:T(8,128)}, u32[]{:S(2)}) copy-start(f32[4,8,8,1024]{3,2,1,0:T(8,128)} %get-tuple-element.34) | copy-start | bytes 3145732

commit v2 on v1

v2 whole, which is shorter than its diff:
```python
import functools

import jax
import jax.numpy as jnp
from jax import lax
from jax.experimental import pallas as pl
from jax.experimental.pallas import tpu as pltpu
from jax.sharding import PartitionSpec as P

BLK = 8
CAP = 2
LANES = 128
MESH = pl.DeviceIdType.MESH
F32 = jnp.float32
BF16 = jnp.bfloat16


def iota(shape, dim):
    return lax.broadcasted_iota(jnp.int32, shape, dim)


def step_kernel(
    groups, subs,
    asked_src, points, pidx_col, pidx_row, sidx_row, l3_row, lrows, cent1, cent2, cent3,
    l1_out, l2_new, l3_out,
    asked, served, fetched, back_src, back_dst, l1_buf,
    l2_src, l2_dst, acc2, mass2, meta_src, meta_dst, w_row,
    a_src, a_dst, b_src, b_dst, c_buf,
    e0s, e0r, e1s, e1r, e3s, e3r, l2s, l2r, ms, mr,
    as_, ar, bs, br, cs, cr, ds_, dr, l1sem, l2sem, lsem,
):
    n = groups * subs
    g_me, s_me = lax.axis_index("grp"), lax.axis_index("sub")
    me = g_me * subs + s_me
    slots = CAP * BLK
    pts, feat = points.shape
    cap = l2_src.shape[1]
    rows_a = a_src.shape[1]
    rows_b = b_src.shape[1]

    def flat(k):
        t = lax.rem(me + k, n)
        return (lax.div(t, subs), lax.rem(t, subs))

    def sub_peer(k):
        return lax.rem(s_me + k, subs)

    def grp_peer(k):
        return lax.rem(g_me + k, groups)

    barrier = pltpu.get_barrier_semaphore()

    @pl.loop(1, n)
    def _(k):
        pl.semaphore_signal(barrier, inc=1, device_id=flat(k), device_id_type=MESH)

    pl.semaphore_wait(barrier, n - 1)

    def remote(src, dst, ss, rs, dev):
        return pltpu.make_async_remote_copy(
            src_ref=src, dst_ref=dst, send_sem=ss, recv_sem=rs, device_id=dev, device_id_type=MESH
        )

    def e0(k):
        t = lax.rem(me + k, n)
        return remote(asked_src.at[t], asked.at[me], e0s.at[k], e0r.at[k], flat(k))

    def e1(k):
        t = lax.rem(me + k, n)
        return remote(served.at[t], fetched.at[me], e1s.at[k], e1r.at[k], flat(k))

    def e3(k):
        t = lax.rem(me + k, n)
        return remote(back_src.at[t], back_dst.at[me], e3s.at[k], e3r.at[k], flat(k))

    def e2(k):
        t = sub_peer(k)
        return remote(l2_src.at[t], l2_dst.at[s_me], l2s.at[k], l2r.at[k], (g_me, t))

    def em(k):
        t = sub_peer(k)
        return remote(meta_src.at[t], meta_dst.at[s_me], ms.at[k], mr.at[k], (g_me, t))

    def ea(k):
        t = grp_peer(k)
        return remote(a_src.at[t], a_dst.at[g_me], as_.at[k], ar.at[k], (t, s_me))

    def eb(k):
        t = sub_peer(k)
        return remote(b_src.at[t], b_dst.at[s_me], bs.at[k], br.at[k], (g_me, t))

    def ec(k):
        t = sub_peer(k)
        return remote(c_buf.at[s_me], c_buf.at[s_me], cs.at[k], cr.at[k], (g_me, t))

    def ed(k):
        t = grp_peer(k)
        return remote(c_buf, l3_out.at[g_me], ds_.at[k], dr.at[k], (t, s_me))

    @pl.loop(1, n)
    def _(k):
        e0(k).start()

    asked[me] = asked_src[me]

    def route(t):
        slot = iota((cap, pts), 0) + t * cap
        return jnp.where(sidx_row[...] == slot, F32(1), F32(0)).astype(BF16)

    def build(k):
        t = sub_peer(k)
        l2_src[t] = jnp.dot(route(t), points[...], preferred_element_type=F32).astype(BF16)

    part = subs // 8
    cuts = [1, 1 + part, 1 + 3 * part, 1 + 4 * part, 1 + 5 * part, subs]

    def send_part(j):
        @pl.loop(cuts[j], cuts[j + 1])
        def _(k):
            e2(k).start()

    def build_part(lo, hi):
        @pl.loop(lo, hi)
        def _(k):
            build(k)

    build_part(cuts[0], cuts[1])
    send_part(0)

    @pl.loop(1, n)
    def _(k):
        e0(k).wait_recv()

    tile = LANES
    total = n * slots
    per = tile // slots
    k1_dev = cent1.shape[0]

    def targets(lo, count):
        tiles = asked[pl.ds(lo, count)]
        pair = jnp.concatenate([tiles[:, :, c : c + 1] for c in range(CAP)], axis=1)
        return pair.reshape(count * slots, 1)

    @pl.loop(0, total // tile)
    def _(i):
        hot = jnp.where(
            targets(i * per, per) == iota((tile, k1_dev), 1), F32(1), F32(0)
        ).astype(BF16)
        rows = jnp.dot(hot, cent1[...], preferred_element_type=F32).astype(BF16)
        served[pl.ds(i * per, per)] = rows.reshape(per, slots, feat)

    @pl.loop(1, n)
    def _(k):
        e1(k).start()

    fetched[me] = served[me]
    build_part(cuts[1], cuts[2])
    send_part(1)
    build_part(cuts[2], subs)
    build(0)
    l2_dst[s_me] = l2_src[s_me]

    @pl.loop(1, n)
    def _(k):
        e1(k).wait_recv()

    @pl.loop(0, pts // tile)
    def _(i):
        at = pl.ds(pl.multiple_of(i * tile, tile), tile)
        hot = jnp.where(pidx_col[at, :] == iota((tile, total), 1), F32(1), F32(0)).astype(BF16)
        near = jnp.dot(hot, fetched[...].reshape(total, feat), preferred_element_type=F32)
        diff = points[at, :].astype(F32) - near
        spread = jnp.sum(diff * diff, axis=1, keepdims=True) / feat
        w = (1.0 / (1.0 + spread)).astype(BF16).astype(F32)
        eye = iota((tile, tile), 0) == iota((tile, tile), 1)
        w_row[:, at] = jnp.sum(jnp.where(eye, w, F32(0)), axis=0, keepdims=True)

    k3 = groups * rows_a
    tile3 = min(tile, rows_a)
    for j in range(k3 // tile3):
        hot = jnp.where(l3_row[...] == iota((tile3, pts), 0) + j * tile3, w_row[...], F32(0))
        m = jnp.sum(hot, axis=1, keepdims=True)
        s = jnp.dot(hot.astype(BF16), points[...], preferred_element_type=F32)
        g, r = (j * tile3) // rows_a, (j * tile3) % rows_a
        a_src[g, r : r + tile3, :feat] = s.astype(BF16)
        a_src[g, r : r + tile3, feat:] = jnp.broadcast_to(m, (tile3, LANES)).astype(BF16)
    for k in range(1, groups):
        ea(k).start()

    meta_rows = jnp.where(iota((8, pts), 0) == 0, w_row[...], lrows[...]).astype(BF16)

    def meta(k):
        t = sub_peer(k)
        meta_src[t] = lax.dot_general(
            meta_rows, route(t), (((1,), (1,)), ((), ())), preferred_element_type=F32
        )

    @pl.loop(0, total // tile)
    def _(i):
        hot = jnp.where(pidx_row[...] == iota((tile, pts), 0) + i * tile, w_row[...], F32(0))
        m = jnp.sum(hot, axis=1, keepdims=True)
        s = jnp.dot(hot.astype(BF16), points[...], preferred_element_type=F32)
        at = pl.ds(i * per, per)
        back_src[at, :, :feat] = s.astype(BF16).reshape(per, slots, feat)
        back_src[at, :, feat:] = (
            jnp.broadcast_to(m, (tile, LANES)).astype(BF16).reshape(per, slots, LANES)
        )

    for k in range(1, groups):
        ea(k).wait_recv()
    a_dst[g_me] = a_src[g_me]
    acc = a_dst[0].astype(F32)
    for j in range(1, groups):
        acc = acc + a_dst[j].astype(F32)
    for j in range(subs):
        b_src[j] = acc[j * rows_b : (j + 1) * rows_b, :]
    for k in range(1, subs):
        eb(k).start()

    @pl.loop(1, n)
    def _(k):
        e3(k).start()

    back_dst[me] = back_src[me]
    send_part(2)

    @pl.loop(1, subs)
    def _(k):
        meta(k)
        em(k).start()

    meta(0)
    meta_dst[s_me] = meta_src[s_me]

    for k in range(1, subs):
        eb(k).wait_recv()
    b_dst[s_me] = b_src[s_me]
    acc = b_dst[0]
    for j in range(1, subs):
        acc = acc + b_dst[j]
    c_buf[s_me] = (cent3[g_me, s_me] + acc[:, :feat]) / (1.0 + acc[:, feat : feat + 1])
    for k in range(1, subs):
        ec(k).start()
    send_part(3)
    send_part(4)

    @pl.loop(1, n)
    def _(k):
        e3(k).wait_recv()

    tile1 = min(2 * tile, k1_dev)

    def l1_copy(i):
        at = pl.ds(pl.multiple_of(i * tile1, tile1), tile1)
        return pltpu.make_async_copy(l1_buf.at[at], l1_out.at[at], l1sem.at[i])

    @pl.loop(0, k1_dev // tile1)
    def _(i):
        at = pl.ds(pl.multiple_of(i * tile1, tile1), tile1)
        hot = jnp.where(
            targets(0, n) == iota((total, tile1), 1) + i * tile1, F32(1), F32(0)
        ).astype(BF16)
        got = lax.dot_general(
            hot,
            back_dst[...].reshape(total, back_dst.shape[2]),
            (((0,), (0,)), ((), ())),
            preferred_element_type=F32,
        )
        l1_buf[at, :] = (cent1[at, :].astype(F32) + got[:, :feat]) / (1.0 + got[:, feat : feat + 1])
        l1_copy(i).start()

    for k in range(1, subs):
        ec(k).wait_recv()
    for k in range(1, groups):
        ed(k).start()
    own_l3 = pltpu.make_async_copy(c_buf, l3_out.at[g_me], lsem)
    own_l3.start()

    @pl.loop(1, subs)
    def _(k):
        em(k).wait_recv()

    rows2 = cent2.shape[0]
    tile2 = min(2 * tile, rows2)
    acc2[...] = jnp.zeros_like(acc2)
    mass2[...] = jnp.zeros_like(mass2)

    def gather2(t):
        label = meta_dst[t, 1:2, :] * 64.0 + meta_dst[t, 2:3, :]
        weight = meta_dst[t, 0:1, :]
        rows = l2_dst[t]

        @pl.loop(0, rows2 // tile2)
        def _(i):
            at = pl.ds(pl.multiple_of(i * tile2, tile2), tile2)
            hot = jnp.where(
                label == (iota((tile2, cap), 0) + i * tile2).astype(F32), weight, F32(0)
            )
            mass2[at, :] += jnp.sum(hot, axis=1, keepdims=True)
            acc2[at, :] += jnp.dot(hot.astype(BF16), rows, preferred_element_type=F32)

    gather2(s_me)

    @pl.loop(1, subs)
    def _(k):
        e2(k).wait_recv()
        gather2(lax.rem(s_me - k + subs, subs))

    def l2_copy(i):
        at = pl.ds(pl.multiple_of(i * tile2, tile2), tile2)
        return pltpu.make_async_copy(acc2.at[at], l2_new.at[at], l2sem.at[i])

    @pl.loop(0, rows2 // tile2)
    def _(i):
        at = pl.ds(pl.multiple_of(i * tile2, tile2), tile2)
        acc2[at, :] = (cent2[at, :].astype(F32) + acc2[at, :]) / (1.0 + mass2[at, :])
        l2_copy(i).start()

    own_l3.wait()
    for k in range(1, groups):
        ed(k).wait_recv()

    @pl.loop(0, k1_dev // tile1)
    def _(i):
        l1_copy(i).wait()

    @pl.loop(0, rows2 // tile2)
    def _(i):
        l2_copy(i).wait()

    @pl.loop(1, n)
    def _(k):
        e0(k).wait_send()
        e1(k).wait_send()
        e3(k).wait_send()

    @pl.loop(1, subs)
    def _(k):
        e2(k).wait_send()
        em(k).wait_send()
        eb(k).wait_send()
        ec(k).wait_send()

    for k in range(1, groups):
        ea(k).wait_send()
        ed(k).wait_send()


def ranks(hits):
    return jnp.sum(jnp.cumsum(hits, axis=0) * hits, axis=1) - 1


def shards(points, level1_ids, level2_ids, level3_ids, needed, centroids1, centroids2, centroids3, *, k2):
    groups, subs = lax.axis_size("grp"), lax.axis_size("sub")
    n = groups * subs
    pts, feat = points.shape
    k1_dev = centroids1.shape[0]
    k3 = centroids3.shape[0]
    blocks_dev = k1_dev // BLK
    slots = CAP * BLK
    need = needed.shape[1]
    wide = feat + LANES

    wanted = needed[0]
    owners = wanted // blocks_dev
    same = owners[:, None] == owners[None, :]
    before = jnp.arange(need)[None, :] < jnp.arange(need)[:, None]
    places = jnp.sum((same & before).astype(jnp.int32), axis=1)
    slot_index = owners * CAP + places
    requests = jnp.sum(
        jnp.where(
            slot_index[None, :] == jnp.arange(n * CAP)[:, None], (wanted % blocks_dev)[None, :], 0
        ),
        axis=1,
    ).reshape(n, 1, CAP)
    asked = jnp.pad(
        requests * BLK + jnp.arange(BLK, dtype=jnp.int32)[None, :, None],
        ((0, 0), (0, 0), (0, LANES - CAP)),
    )

    entry = level1_ids // BLK
    point_slots = jnp.sum(
        jnp.where(entry[:, None] == jnp.arange(need)[None, :], slot_index[None, :], 0), axis=1
    )
    row_index = point_slots * BLK + level1_ids % BLK

    shard_rows = k2 // subs
    cap = 2 * pts // subs
    range_of = level2_ids // shard_rows
    hits = (range_of[:, None] == jnp.arange(subs)[None, :]).astype(jnp.int32)
    send_index = range_of * cap + ranks(hits)
    local = level2_ids % shard_rows
    lrows = (
        jnp.zeros((8, pts), F32)
        .at[1].set((local // 64).astype(F32))
        .at[2].set((local % 64).astype(F32))
    )

    rows_a = k3 // groups
    rows_b = rows_a // subs
    cent3 = centroids3.astype(F32).reshape(groups, subs, rows_b, feat)
    vmem = pl.BlockSpec(memory_space=pltpu.VMEM)
    anywhere = pl.BlockSpec(memory_space=pl.ANY)
    dma = pltpu.SemaphoreType.DMA
    l1, l2, l3 = pl.pallas_call(
        functools.partial(step_kernel, groups, subs),
        out_shape=(
            jax.ShapeDtypeStruct((k1_dev, feat), F32),
            jax.ShapeDtypeStruct((shard_rows, feat), F32),
            jax.ShapeDtypeStruct((groups, subs, rows_b, feat), F32),
        ),
        in_specs=[vmem] * 10,
        out_specs=[anywhere] * 3,
        scratch_shapes=[
            pltpu.VMEM((n, BLK, LANES), jnp.int32),
            pltpu.VMEM((n, slots, feat), BF16),
            pltpu.VMEM((n, slots, feat), BF16),
            pltpu.VMEM((n, slots, wide), BF16),
            pltpu.VMEM((n, slots, wide), BF16),
            pltpu.VMEM((k1_dev, feat), F32),
            pltpu.VMEM((subs, cap, feat), BF16),
            pltpu.VMEM((subs, cap, feat), BF16),
            pltpu.VMEM((shard_rows, feat), F32),
            pltpu.VMEM((shard_rows, 1), F32),
            pltpu.VMEM((subs, 8, cap), F32),
            pltpu.VMEM((subs, 8, cap), F32),
            pltpu.VMEM((1, pts), F32),
            pltpu.VMEM((groups, rows_a, wide), BF16),
            pltpu.VMEM((groups, rows_a, wide), BF16),
            pltpu.VMEM((subs, rows_b, wide), F32),
            pltpu.VMEM((subs, rows_b, wide), F32),
            pltpu.VMEM((subs, rows_b, feat), F32),
            dma((n,)), dma((n,)), dma((n,)), dma((n,)), dma((n,)), dma((n,)),
            dma((subs,)), dma((subs,)), dma((subs,)), dma((subs,)),
            dma((groups,)), dma((groups,)),
            dma((subs,)), dma((subs,)), dma((subs,)), dma((subs,)),
            dma((groups,)), dma((groups,)),
            dma((k1_dev // 256,)), dma((shard_rows // 256,)), dma,
        ],
        compiler_params=pltpu.CompilerParams(
            collective_id=0, has_side_effects=True, vmem_limit_bytes=60 * 1024 * 1024
        ),
        name="step",
    )(
        asked,
        points,
        row_index[:, None],
        row_index[None, :],
        send_index[None, :],
        level3_ids[None, :],
        lrows,
        centroids1,
        centroids2[0],
        cent3,
    )
    return l1, l2[None], l3.reshape(k3, feat)


def solution(mesh):
    placed = (
        P(("grp", "sub"), None),
        P(("grp", "sub")),
        P(("grp", "sub")),
        P(("grp", "sub")),
        P(("grp", "sub"), None),
        P(("grp", "sub"), None),
        P("grp", "sub", None),
        P(),
    )

    def run(*args):
        return jax.shard_map(
            functools.partial(shards, k2=args[6].shape[1]),
            mesh=mesh,
            in_specs=placed,
            out_specs=(P(("grp", "sub"), None), P("grp", "sub", None), P()),
            check_vma=False,
        )(*args)

    return run
```

time: 255 us -> 222 us (0.87)
  the two profiles are of different devices: /device:TPU:1 before, /device:TPU:31 now
where the time goes in v2:
time: 222 us; the launch traced here: 221 us
  Pallas kernels  198 us (89%)
  local copies, waits for them, and re-layouts  13.8 us (6%)
  other arithmetic  9.09 us (4%)
    pallas_call x1, Pallas kernels, shards(): pl.pallas_call(functools.partial(step_kernel, groups, subs), out_shape=(j...  198 us
    unnamed x11, local copies, waits for them, and re-layouts  11.6 us

profile of v2, /device:TPU:31, one launch (start us, length us, event | category | flops | bytes accessed | tf_op | source)
XLA Modules:
  0.0 221.4 jit_solution(2404621657012540369)
XLA Ops:
  0.6 0.7 and_select_fusion.1
  1.3 0.7 and_select_fusion.2
  2.0 0.2 convert_reduce_fusion
  2.1 0.1 select_reduce_fusion.1
  2.3 0.7 add_select_fusion.5
  3.0 0.1 select_reduce_fusion
  3.0 0.7 fusion.4
  3.7 0.0 copy-start.3
  3.7 0.7 fusion.6
  4.5 0.1 mul.38
  4.6 0.1 scatter.9.lrows
  4.7 0.0 copy-start.2
  4.7 2.3 %reduce-window.6 = s32[8,8,128]{2,1,0:T(8,128)S(1)} reduce-window(s32[8,8,128]{2,1,0:T(8,128)S(1)} %fusion.2, s32[]{:T(128)} %constant.144.clone.1), window={size=1x1x128 pad=0_0x0_0x127_0}, to_apply=%region_3.4 | reduce-window | flops 1040384 | bytes 65540 | tf_op jit(solution)/shard_map/reduce-window | solution.py:472
  7.0 0.3 slice_reduce_fusion
  7.3 0.2 reduce-window.9
  7.4 0.1 add_bitcast_fusion
  7.5 0.6 add_add_fusion
  8.2 0.7 pad.9.asked_src
  8.8 1.0 copy.12.pidx_col
  9.8 2.1 convert.1.cent3
  12.0 0.0 copy-done.3
  12.0 0.0 copy-done.2
  12.0 197.8 %step.1 = (f32[2048,1024]{1,0:T(8,128)}, f32[1024,1024]{1,0:T(8,128)}, f32[4,8,8,1024]{3,2,1,0:T(8,128)}) custom-call(s32[32,8,128]{2,1,0:T(8,128)} %pad.9.asked_src, bf16[1024,1024]{1,0:T(8,128)(2,1)} %points.1, s32[1024,1]{1,0:T(8,128)} %copy.12.pidx_col, s32[1,1024]{1,0:T(1,128)} %bitcast.50, s32[1,1024]{1,0:T(1,128)} %bitcast.51, s32[1,1024]{1,0:T(1,128)} %bitcast.55, ...), custom_call_target="tpu_custom_call" | custom-call | tf_op jit(solution)/shard_map/step/pallas_call | solution.py:405
  209.8 0.0 copy-start
  209.8 8.6 %copy.19 = f32[2048,1024]{1,0:T(8,128)} copy(f32[2048,1024]{1,0:T(8,128)} %get-tuple-element.41) | data formatting | bytes 16777216
  218.4 0.0 copy-done
  218.4 0.0 copy-start.1
  218.4 2.0 copy.20
  220.5 0.0 copy-done.1
  220.5 1.0 copy.21
  (6 shorter events, 0.1 us)
Async XLA Ops:
  3.7 8.2 %copy-start.3 = (s32[1024]{0:T(1024)}, s32[1024]{0:T(1024)S(1)}, u32[]{:S(2)}) copy-start(s32[1024]{0:T(1024)S(1)} %fusion.4) | copy-start | bytes 12292
  4.7 7.3 %copy-start.2 = (f32[8,1024]{1,0:T(8,128)}, f32[8,1024]{1,0:T(8,128)S(1)}, u32[]{:S(2)}) copy-start(f32[8,1024]{1,0:T(8,128)S(1)} %scatter.9.lrows) | copy-start | bytes 98308
  209.8 8.6 %copy-start = (f32[1024,1024]{1,0:T(8,128)S(1)}, f32[1024,1024]{1,0:T(8,128)}, u32[]{:S(2)}) copy-start(f32[1024,1024]{1,0:T(8,128)} %get-tuple-element.31) | copy-start | bytes 12582916
  218.4 2.0 copy-start.1

commit v3 on v2

--- a/solution.py
+++ b/solution.py
@@ -42,8 +42,20 @@
         t = lax.rem(me + k, n)
         return (lax.div(t, subs), lax.rem(t, subs))
 
+    half = subs // 2
+
+    def side(k):
+        local = lax.div(k, half + 1)
+        base = lax.rem(lax.div(s_me, half) + 1 - local, 2) * half
+        return base, k - 1 - local * (half - 1)
+
     def sub_peer(k):
-        return lax.rem(s_me + k, subs)
+        base, j = side(k)
+        return base + lax.rem(lax.rem(s_me, half) + j, half)
+
+    def sub_source(k):
+        base, j = side(k)
+        return base + lax.rem(lax.rem(s_me, half) + half - j, half)
 
     def grp_peer(k):
         return lax.rem(g_me + k, groups)
@@ -107,24 +119,28 @@
         slot = iota((cap, pts), 0) + t * cap
         return jnp.where(sidx_row[...] == slot, F32(1), F32(0)).astype(BF16)
 
-    def build(k):
-        t = sub_peer(k)
+    def build(t):
         l2_src[t] = jnp.dot(route(t), points[...], preferred_element_type=F32).astype(BF16)
 
     part = subs // 8
-    cuts = [1, 1 + part, 1 + 3 * part, 1 + 4 * part, 1 + 5 * part, subs]
+    parts = [
+        (1, 1 + part),
+        (1 + part, 1 + 2 * part),
+        (half + 1, subs),
+        (1 + 2 * part, half + 1),
+    ]
 
     def send_part(j):
-        @pl.loop(cuts[j], cuts[j + 1])
+        @pl.loop(*parts[j])
         def _(k):
             e2(k).start()
 
     def build_part(lo, hi):
         @pl.loop(lo, hi)
         def _(k):
-            build(k)
-
-    build_part(cuts[0], cuts[1])
+            build(sub_peer(k))
+
+    build_part(*parts[0])
     send_part(0)
 
     @pl.loop(1, n)
@@ -154,10 +170,10 @@
         e1(k).start()
 
     fetched[me] = served[me]
-    build_part(cuts[1], cuts[2])
+    build_part(*parts[1])
     send_part(1)
-    build_part(cuts[2], subs)
-    build(0)
+    build_part(1 + 2 * part, subs)
+    build(s_me)
     l2_dst[s_me] = l2_src[s_me]
 
     @pl.loop(1, n)
@@ -189,8 +205,7 @@
 
     meta_rows = jnp.where(iota((8, pts), 0) == 0, w_row[...], lrows[...]).astype(BF16)
 
-    def meta(k):
-        t = sub_peer(k)
+    def meta(t):
         meta_src[t] = lax.dot_general(
             meta_rows, route(t), (((1,), (1,)), ((), ())), preferred_element_type=F32
         )
@@ -213,7 +228,7 @@
     for j in range(1, groups):
         acc = acc + a_dst[j].astype(F32)
     for j in range(subs):
-        b_src[j] = acc[j * rows_b : (j + 1) * rows_b, :]
+        b_src[j] = acc[j * rows_b : (j + 1) * rows_b, :].astype(BF16)
     for k in range(1, subs):
         eb(k).start()
 
@@ -226,23 +241,22 @@
 
     @pl.loop(1, subs)
     def _(k):
-        meta(k)
+        meta(sub_peer(k))
         em(k).start()
 
-    meta(0)
+    meta(s_me)
     meta_dst[s_me] = meta_src[s_me]
 
     for k in range(1, subs):
         eb(k).wait_recv()
     b_dst[s_me] = b_src[s_me]
-    acc = b_dst[0]
+    acc = b_dst[0].astype(F32)
     for j in range(1, subs):
-        acc = acc + b_dst[j]
+        acc = acc + b_dst[j].astype(F32)
     c_buf[s_me] = (cent3[g_me, s_me] + acc[:, :feat]) / (1.0 + acc[:, feat : feat + 1])
     for k in range(1, subs):
         ec(k).start()
     send_part(3)
-    send_part(4)
 
     @pl.loop(1, n)
     def _(k):
@@ -266,7 +280,8 @@
             (((0,), (0,)), ((), ())),
             preferred_element_type=F32,
         )
-        l1_buf[at, :] = (cent1[at, :].astype(F32) + got[:, :feat]) / (1.0 + got[:, feat : feat + 1])
+        new = (cent1[at, :].astype(F32) + got[:, :feat]) / (1.0 + got[:, feat : feat + 1])
+        l1_buf[at, :] = new.astype(BF16)
         l1_copy(i).start()
 
     for k in range(1, subs):
@@ -301,10 +316,12 @@
 
     gather2(s_me)
 
-    @pl.loop(1, subs)
-    def _(k):
-        e2(k).wait_recv()
-        gather2(lax.rem(s_me - k + subs, subs))
+    for span in parts:
+
+        @pl.loop(*span)
+        def _(k):
+            e2(k).wait_recv()
+            gather2(sub_source(k))
 
     def l2_copy(i):
         at = pl.ds(pl.multiple_of(i * tile2, tile2), tile2)
@@ -405,7 +422,7 @@
     l1, l2, l3 = pl.pallas_call(
         functools.partial(step_kernel, groups, subs),
         out_shape=(
-            jax.ShapeDtypeStruct((k1_dev, feat), F32),
+            jax.ShapeDtypeStruct((k1_dev, feat), BF16),
             jax.ShapeDtypeStruct((shard_rows, feat), F32),
             jax.ShapeDtypeStruct((groups, subs, rows_b, feat), F32),
         ),
@@ -417,7 +434,7 @@
             pltpu.VMEM((n, slots, feat), BF16),
             pltpu.VMEM((n, slots, wide), BF16),
             pltpu.VMEM((n, slots, wide), BF16),
-            pltpu.VMEM((k1_dev, feat), F32),
+            pltpu.VMEM((k1_dev, feat), BF16),
             pltpu.VMEM((subs, cap, feat), BF16),
             pltpu.VMEM((subs, cap, feat), BF16),
             pltpu.VMEM((shard_rows, feat), F32),
@@ -427,8 +444,8 @@
             pltpu.VMEM((1, pts), F32),
             pltpu.VMEM((groups, rows_a, wide), BF16),
             pltpu.VMEM((groups, rows_a, wide), BF16),
-            pltpu.VMEM((subs, rows_b, wide), F32),
-            pltpu.VMEM((subs, rows_b, wide), F32),
+            pltpu.VMEM((subs, rows_b, wide), BF16),
+            pltpu.VMEM((subs, rows_b, wide), BF16),
             pltpu.VMEM((subs, rows_b, feat), F32),
             dma((n,)), dma((n,)), dma((n,)), dma((n,)), dma((n,)), dma((n,)),
             dma((subs,)), dma((subs,)), dma((subs,)), dma((subs,)),
@@ -453,7 +470,7 @@
         centroids2[0],
         cent3,
     )
-    return l1, l2[None], l3.reshape(k3, feat)
+    return l1.astype(F32), l2[None], l3.reshape(k3, feat)
 
 
 def solution(mesh):

time: 222 us -> 193 us (0.87)
  the two profiles are of different devices: /device:TPU:31 before, /device:TPU:1 now
where the time goes in v3:
time: 193 us
  Pallas kernels  171 us (89%)
  other arithmetic  15.9 us (8%)
  local copies, waits for them, and re-layouts  5.18 us (3%)
    pallas_call x1, Pallas kernels, shards(): pl.pallas_call(functools.partial(step_kernel, groups, subs), out_shape=(j...  171 us
    convert_element_type x1, other arithmetic, shards(): return (l1.astype(F32), l2[None], l3.reshape(k3, feat))  6.79 us

profile of v3, /device:TPU:1, one launch (start us, length us, event | category | flops | bytes accessed | tf_op | source)
XLA Modules:
  0.0 193.0 jit_solution(17824725750363814627)
XLA Ops:
  0.6 0.7 and_select_fusion.1
  1.3 0.7 and_select_fusion.2
  2.0 0.2 convert_reduce_fusion
  2.1 0.1 select_reduce_fusion.1
  2.3 0.7 add_select_fusion.5
  3.0 0.1 select_reduce_fusion
  3.0 0.7 fusion.4
  3.7 0.0 copy-start.3
  3.7 0.7 fusion.6
  4.5 0.1 mul.38
  4.6 0.1 scatter.9.lrows
  4.7 0.0 copy-start.2
  4.7 2.3 %reduce-window.6 = s32[8,8,128]{2,1,0:T(8,128)S(1)} reduce-window(s32[8,8,128]{2,1,0:T(8,128)S(1)} %fusion.2, s32[]{:T(128)} %constant.144.clone.1), window={size=1x1x128 pad=0_0x0_0x127_0}, to_apply=%region_3.4 | reduce-window | flops 1040384 | bytes 65540 | tf_op jit(solution)/shard_map/reduce-window | solution.py:489
  7.0 0.3 slice_reduce_fusion
  7.3 0.2 reduce-window.9
  7.4 0.1 add_bitcast_fusion
  7.5 0.6 add_add_fusion
  8.1 0.7 pad.9.asked_src
  8.8 1.0 copy.12.pidx_col
  9.8 2.1 %convert.1.cent3 = f32[4,8,8,1024]{3,2,1,0:T(8,128)} convert(bf16[4,8,8,1024]{3,2,1,0:T(8,128)(2,1)} %bitcast.47) | non-fusion elementwise | flops 262144 | bytes 1572864 | tf_op jit(solution)/shard_map/reshape | solution.py:418
  12.0 0.0 copy-done.3
  12.0 0.0 copy-done.2
  12.0 171.3 %step.1 = (bf16[2048,1024]{1,0:T(8,128)(2,1)}, f32[1024,1024]{1,0:T(8,128)}, f32[4,8,8,1024]{3,2,1,0:T(8,128)}) custom-call(s32[32,8,128]{2,1,0:T(8,128)} %pad.9.asked_src, bf16[1024,1024]{1,0:T(8,128)(2,1)} %points.1, s32[1024,1]{1,0:T(8,128)} %copy.12.pidx_col, s32[1,1024]{1,0:T(1,128)} %bitcast.50, s32[1,1024]{1,0:T(1,128)} %bitcast.51, ...), custom_call_target="tpu_custom_call" | custom-call | tf_op jit(solution)/shard_map/step/pallas_call | solution.py:422
  183.2 0.0 copy-start
  183.2 6.8 %convert_element_type.22 = f32[2048,1024]{1,0:T(8,128)} convert(bf16[2048,1024]{1,0:T(8,128)(2,1)} %get-tuple-element.30) | non-fusion elementwise | flops 2097152 | bytes 12582912 | tf_op jit(solution)/shard_map/convert_element_type | solution.py:473
  190.0 0.0 copy-done
  190.0 0.0 copy-start.1
  190.0 2.0 %copy.18 = f32[1,1024,1024]{2,1,0:T(8,128)} copy(f32[1,1024,1024]{2,1,0:T(8,128)S(1)} %bitcast.44) | data formatting | bytes 8388608
  192.1 0.0 copy-done.1
  192.1 1.0 copy.19
  (6 shorter events, 0.1 us)
Async XLA Ops:
  3.7 8.2 %copy-start.3 = (s32[1024]{0:T(1024)}, s32[1024]{0:T(1024)S(1)}, u32[]{:S(2)}) copy-start(s32[1024]{0:T(1024)S(1)} %fusion.4) | copy-start | bytes 12292
  4.7 7.3 %copy-start.2 = (f32[8,1024]{1,0:T(8,128)}, f32[8,1024]{1,0:T(8,128)S(1)}, u32[]{:S(2)}) copy-start(f32[8,1024]{1,0:T(8,128)S(1)} %scatter.9.lrows) | copy-start | bytes 98308
  183.2 6.8 %copy-start = (f32[1024,1024]{1,0:T(8,128)S(1)}, f32[1024,1024]{1,0:T(8,128)}, u32[]{:S(2)}) copy-start(f32[1024,1024]{1,0:T(8,128)} %get-tuple-element.31) | copy-start | bytes 12582916
  190.0 2.0 %copy-start.1 = (f32[4,8,8,1024]{3,2,1,0:T(8,128)S(1)}, f32[4,8,8,1024]{3,2,1,0:T(8,128)}, u32[]{:S(2)}) copy-start(f32[4,8,8,1024]{3,2,1,0:T(8,128)} %get-tuple-element.32) | copy-start | bytes 3145732
